TPU v7x, 256 devices: a whole 4x4x8 slice. The times are simulated.
256 devices in a mesh: blk: 8 (over x_hi, y), group: 32 (over z, x_lo, core).
Axes of the slice: x: 4 (x_hi: 2, x_lo: 2; x = x_hi * 2 + x_lo), y: 4, z: 8, core: 2. Of those that a mesh axis runs over, the one named last changes fastest.
Arguments:
- walk_rows: bfloat16 [4096, 131072], P('blk', 'group'), may hold values from -6 to 6
- col_values: bfloat16 [49152, 4096], P('group', 'blk'), may hold values from -0.02734375 to 0.02734375
- col_index: int32 [96, 8], P('group'), may hold values from 0 to 7
- col_count: int32 [32, 8], P('group'), may hold values from 1 to 3, as said below
Outputs:
- inflated: float32 [4096, 4096], P(('blk', 'group'))
Inputs may be any that keep to these rules, and one draw needn't show every extreme that they name: `col_count`: each list holds 1 to 3 valid slots; some list holds 3; contents of the other slots are arbitrary.
All inputs are finite; a program needn't handle non-finite values.
Results may differ from a plain program's by a relative error of at most 0.0003.
Values may be sent and summed in bfloat16 or wider, within the bound.
No kernel may reach another device: no remote copies, remote signals or barrier semaphores. Data moves between devices by JAX's collectives and lax.ppermute only.
A program may use at most 64 MiB of HBM per device.

v0:
```python
import jax
import jax.numpy as jnp
from jax import lax
from jax.sharding import PartitionSpec as P


def shifted(shard, axis, by):
    size = lax.axis_size(axis)
    return lax.ppermute(shard, axis, [(i, (i + by) % size) for i in range(size)])


def on_device(walk_rows, col_values, col_index, col_count):
    width = col_values.shape[1]
    slots = col_values.shape[0] // width
    nblock = lax.axis_size("blk")
    myself = lax.axis_index("blk")
    rows_here = walk_rows.shape[0]
    share = rows_here // lax.axis_size("group")

    def panel_product(rows, values, panel):
        index = lax.dynamic_slice_in_dim(col_index, panel, 1, 1)[:, 0]
        count = lax.dynamic_slice_in_dim(col_count, panel, 1, 1)[0, 0]
        total = jnp.zeros((rows.shape[0], width), jnp.float32)
        for slot in range(slots):
            block = lax.dynamic_slice_in_dim(rows, index[slot] * width, width, 1)
            piece = values[slot * width : (slot + 1) * width]
            product = jnp.dot(block, piece, preferred_element_type=jnp.float32)
            total = total + jnp.where(slot < count, product, jnp.zeros_like(product))
        return total

    def turn(step, carry):
        values, result = carry
        panel = (myself - step) % nblock
        part = panel_product(walk_rows, values, panel)
        reduced = lax.psum_scatter(part, "group", scatter_dimension=0, tiled=True)
        result = lax.dynamic_update_slice_in_dim(result, reduced, panel * width, 1)
        values = shifted(values, "blk", 1)
        return (values, result)

    start_out = jnp.zeros((share, nblock * width), jnp.float32)
    unused, expanded = lax.fori_loop(0, nblock, turn, (col_values, start_out))
    squared = expanded * expanded
    column = jnp.sum(squared, axis=0)
    total = lax.psum(column, ("blk", "group"))
    scale = total / (nblock * rows_here) + 1e-06
    return squared / scale


def solution(mesh):
    return jax.shard_map(
        on_device,
        mesh=mesh,
        in_specs=(P("blk", "group"), P("group", "blk"), P("group", None), P("group", None)),
        out_specs=P(("blk", "group"), None),
        check_vma=False,
    )
```

profile of v0, /device:TPU:1, one launch (start us, length us, event | category | flops | bytes accessed | tf_op | source)
XLA Modules:
  0.0 1125.3 jit_solution(7067308069750690020)
XLA Ops:
  6.6 1.4 copy-done
  7.9 1030.1 %while.17 = (s32[]{:T(128)}, bf16[1536,512]{1,0:T(8,128)(2,1)S(1)}, f32[16,4096]{1,0:T(8,128)S(1)}, s32[]{:T(128)}, s32[1,8]{1,0:T(1,128)S(1)}, /*index=5*/s32[3...) while((s32[]{:T(128)}, bf16[1536,512]{1,0:T(8,128)(2,1)S(1)}, ...), condition=%wide.region_2.3_spmd, body=%wide.region_0.2_spmd.sunk | while | flops 806617088 | bytes 21137560 | solution.py:41
  10.5 0.7 fusion.29
  12.4 2.1 convolution_select_fusion.5
  14.5 1.5 convolution_select_fusion.6
  16.0 2.5 fusion.30
  18.5 2.2 collective-permute-start
  20.7 117.8 %reduce-scatter.2.cloned.1.call-done = f32[16,512]{1,0:T(8,128)} async-done(((f32[512,512]{1,0:T(8,128)}), f32[16,512]{1,0:T(8,128)}) %reduce-scatter.2.cloned.1.call-update) | async-done | bytes 32784 | tf_op jit(solution)/shard_map/while/body/eval_jaxpr/reduce_scatter | solution.py:35
  138.5 0.8 constant_dynamic-update-slice_fusion.2
  143.7 2.1 convolution_select_fusion.5
  145.8 1.5 convolution_select_fusion.6
  147.3 2.5 fusion.30
  149.9 117.1 %reduce-scatter.2.cloned.1.call-done = f32[16,512]{1,0:T(8,128)} async-done(((f32[512,512]{1,0:T(8,128)}), f32[16,512]{1,0:T(8,128)}) %reduce-scatter.2.cloned.1.call-update) | async-done | bytes 32784 | tf_op jit(solution)/shard_map/while/body/eval_jaxpr/reduce_scatter | solution.py:35
  267.0 0.8 constant_dynamic-update-slice_fusion.2
  272.2 2.1 convolution_select_fusion.5
  274.3 1.5 convolution_select_fusion.6
  275.8 2.5 fusion.30
  278.4 116.7 %reduce-scatter.2.cloned.1.call-done = f32[16,512]{1,0:T(8,128)} async-done(((f32[512,512]{1,0:T(8,128)}), f32[16,512]{1,0:T(8,128)}) %reduce-scatter.2.cloned.1.call-update) | async-done | bytes 32784 | tf_op jit(solution)/shard_map/while/body/eval_jaxpr/reduce_scatter | solution.py:35
  395.1 0.8 constant_dynamic-update-slice_fusion.2
  400.4 2.1 convolution_select_fusion.5
  402.5 1.5 convolution_select_fusion.6
  404.0 2.5 fusion.30
  406.6 116.8 %reduce-scatter.2.cloned.1.call-done = f32[16,512]{1,0:T(8,128)} async-done(((f32[512,512]{1,0:T(8,128)}), f32[16,512]{1,0:T(8,128)}) %reduce-scatter.2.cloned.1.call-update) | async-done | bytes 32784 | tf_op jit(solution)/shard_map/while/body/eval_jaxpr/reduce_scatter | solution.py:35
  523.4 0.8 constant_dynamic-update-slice_fusion.2
  526.8 0.7 fusion.29
  528.7 2.1 convolution_select_fusion.5
  530.8 1.5 convolution_select_fusion.6
  532.3 2.5 fusion.30
  535.0 116.8 %reduce-scatter.2.cloned.1.call-done = f32[16,512]{1,0:T(8,128)} async-done(((f32[512,512]{1,0:T(8,128)}), f32[16,512]{1,0:T(8,128)}) %reduce-scatter.2.cloned.1.call-update) | async-done | bytes 32784 | tf_op jit(solution)/shard_map/while/body/eval_jaxpr/reduce_scatter | solution.py:35
  651.9 0.8 constant_dynamic-update-slice_fusion.2
  657.1 2.1 convolution_select_fusion.5
  659.2 1.5 convolution_select_fusion.6
  660.7 2.5 fusion.30
  663.5 116.9 %reduce-scatter.2.cloned.1.call-done = f32[16,512]{1,0:T(8,128)} async-done(((f32[512,512]{1,0:T(8,128)}), f32[16,512]{1,0:T(8,128)}) %reduce-scatter.2.cloned.1.call-update) | async-done | bytes 32784 | tf_op jit(solution)/shard_map/while/body/eval_jaxpr/reduce_scatter | solution.py:35
  780.3 0.8 constant_dynamic-update-slice_fusion.2
  785.6 2.1 convolution_select_fusion.5
  787.7 1.5 convolution_select_fusion.6
  789.2 2.5 fusion.30
  791.9 116.9 %reduce-scatter.2.cloned.1.call-done = f32[16,512]{1,0:T(8,128)} async-done(((f32[512,512]{1,0:T(8,128)}), f32[16,512]{1,0:T(8,128)}) %reduce-scatter.2.cloned.1.call-update) | async-done | bytes 32784 | tf_op jit(solution)/shard_map/while/body/eval_jaxpr/reduce_scatter | solution.py:35
  908.8 0.8 constant_dynamic-update-slice_fusion.2
  912.1 0.7 fusion.29
  914.0 2.1 convolution_select_fusion.5
  916.1 1.5 convolution_select_fusion.6
  917.6 2.5 fusion.30
  920.6 116.6 %reduce-scatter.2.cloned.1.call-done = f32[16,512]{1,0:T(8,128)} async-done(((f32[512,512]{1,0:T(8,128)}), f32[16,512]{1,0:T(8,128)}) %reduce-scatter.2.cloned.1.call-update) | async-done | bytes 32784 | tf_op jit(solution)/shard_map/while/body/eval_jaxpr/reduce_scatter | solution.py:35
  1037.3 0.8 constant_dynamic-update-slice_fusion.2
  1038.1 79.7 %psum.7 = f32[4096]{0:T(1024)S(1)} all-reduce(f32[4096]{0:T(1024)S(1)} %multiply_reduce_fusion), channel_id=1, replica_groups=mesh['blk'=8,'group'=32] {'blk','group'}, use_global_device_ids=true, to_apply=%region_4.5 | all-reduce | flops 4096 | bytes 32768 | tf_op jit(solution)/shard_map/psum | solution.py:44
  1117.7 0.7 multiply_divide_fusion
  (68 shorter events, 11.2 us)
Async XLA Ops:
  6.5 1.4 copy-start
  6.5 1.4 copy-start.1
  6.5 1.4 copy-start.2
  7.9 130.5 %reduce-scatter.2.cloned.1.call-start = ((), (), s32[]{:S(2)}) async-start(), calls=%async_computation.1 | async-start | bytes 1081344 | tf_op jit(solution)/shard_map/while/body/eval_jaxpr/reduce_scatter | solution.py:35
  18.5 120.8 %collective-permute-start = (bf16[1536,512]{1,0:T(8,128)(2,1)S(1)}, bf16[1536,512]{1,0:T(8,128)(2,1)S(1)}, u32[]{:S(2)}, u32[]{:S(2)}) collective-permute-start(bf16[1536,512]{1,0:T(8,128)(2,1)S(1)} %copy.10), channel_id=1, source_target_pairs={{0,32},{32,64},{64,96},{96,128},{128,160},{160,192},{192,224},{224... | collective-permute-start | bytes 4718600 | tf_op jit(solution)/shard_map/while/body/eval_jaxpr/ppermute | solution.py:9
  139.3 127.7 %reduce-scatter.2.cloned.1.call-start = ((), (), s32[]{:S(2)}) async-start(), calls=%async_computation.1 | async-start | bytes 1081344 | tf_op jit(solution)/shard_map/while/body/eval_jaxpr/reduce_scatter | solution.py:35
  149.8 117.9 %collective-permute-start = (bf16[1536,512]{1,0:T(8,128)(2,1)S(1)}, bf16[1536,512]{1,0:T(8,128)(2,1)S(1)}, u32[]{:S(2)}, u32[]{:S(2)}) collective-permute-start(bf16[1536,512]{1,0:T(8,128)(2,1)S(1)} %copy.10), channel_id=1, source_target_pairs={{0,32},{32,64},{64,96},{96,128},{128,160},{160,192},{192,224},{224... | collective-permute-start | bytes 4718600 | tf_op jit(solution)/shard_map/while/body/eval_jaxpr/ppermute | solution.py:9
  267.7 127.4 %reduce-scatter.2.cloned.1.call-start = ((), (), s32[]{:S(2)}) async-start(), calls=%async_computation.1 | async-start | bytes 1081344 | tf_op jit(solution)/shard_map/while/body/eval_jaxpr/reduce_scatter | solution.py:35
  278.3 117.6 %collective-permute-start = (bf16[1536,512]{1,0:T(8,128)(2,1)S(1)}, bf16[1536,512]{1,0:T(8,128)(2,1)S(1)}, u32[]{:S(2)}, u32[]{:S(2)}) collective-permute-start(bf16[1536,512]{1,0:T(8,128)(2,1)S(1)} %copy.10), channel_id=1, source_target_pairs={{0,32},{32,64},{64,96},{96,128},{128,160},{160,192},{192,224},{224... | collective-permute-start | bytes 4718600 | tf_op jit(solution)/shard_map/while/body/eval_jaxpr/ppermute | solution.py:9
  395.9 127.5 %reduce-scatter.2.cloned.1.call-start = ((), (), s32[]{:S(2)}) async-start(), calls=%async_computation.1 | async-start | bytes 1081344 | tf_op jit(solution)/shard_map/while/body/eval_jaxpr/reduce_scatter | solution.py:35
  406.4 117.8 %collective-permute-start = (bf16[1536,512]{1,0:T(8,128)(2,1)S(1)}, bf16[1536,512]{1,0:T(8,128)(2,1)S(1)}, u32[]{:S(2)}, u32[]{:S(2)}) collective-permute-start(bf16[1536,512]{1,0:T(8,128)(2,1)S(1)} %copy.10), channel_id=1, source_target_pairs={{0,32},{32,64},{64,96},{96,128},{128,160},{160,192},{192,224},{224... | collective-permute-start | bytes 4718600 | tf_op jit(solution)/shard_map/while/body/eval_jaxpr/ppermute | solution.py:9
  524.2 127.7 %reduce-scatter.2.cloned.1.call-start = ((), (), s32[]{:S(2)}) async-start(), calls=%async_computation.1 | async-start | bytes 1081344 | tf_op jit(solution)/shard_map/while/body/eval_jaxpr/reduce_scatter | solution.py:35
  534.8 117.9 %collective-permute-start = (bf16[1536,512]{1,0:T(8,128)(2,1)S(1)}, bf16[1536,512]{1,0:T(8,128)(2,1)S(1)}, u32[]{:S(2)}, u32[]{:S(2)}) collective-permute-start(bf16[1536,512]{1,0:T(8,128)(2,1)S(1)} %copy.10), channel_id=1, source_target_pairs={{0,32},{32,64},{64,96},{96,128},{128,160},{160,192},{192,224},{224... | collective-permute-start | bytes 4718600 | tf_op jit(solution)/shard_map/while/body/eval_jaxpr/ppermute | solution.py:9
  652.6 127.7 %reduce-scatter.2.cloned.1.call-start = ((), (), s32[]{:S(2)}) async-start(), calls=%async_computation.1 | async-start | bytes 1081344 | tf_op jit(solution)/shard_map/while/body/eval_jaxpr/reduce_scatter | solution.py:35
  663.2 117.9 %collective-permute-start = (bf16[1536,512]{1,0:T(8,128)(2,1)S(1)}, bf16[1536,512]{1,0:T(8,128)(2,1)S(1)}, u32[]{:S(2)}, u32[]{:S(2)}) collective-permute-start(bf16[1536,512]{1,0:T(8,128)(2,1)S(1)} %copy.10), channel_id=1, source_target_pairs={{0,32},{32,64},{64,96},{96,128},{128,160},{160,192},{192,224},{224... | collective-permute-start | bytes 4718600 | tf_op jit(solution)/shard_map/while/body/eval_jaxpr/ppermute | solution.py:9
  781.1 127.7 %reduce-scatter.2.cloned.1.call-start = ((), (), s32[]{:S(2)}) async-start(), calls=%async_computation.1 | async-start | bytes 1081344 | tf_op jit(solution)/shard_map/while/body/eval_jaxpr/reduce_scatter | solution.py:35
  791.7 117.9 %collective-permute-start = (bf16[1536,512]{1,0:T(8,128)(2,1)S(1)}, bf16[1536,512]{1,0:T(8,128)(2,1)S(1)}, u32[]{:S(2)}, u32[]{:S(2)}) collective-permute-start(bf16[1536,512]{1,0:T(8,128)(2,1)S(1)} %copy.10), channel_id=1, source_target_pairs={{0,32},{32,64},{64,96},{96,128},{128,160},{160,192},{192,224},{224... | collective-permute-start | bytes 4718600 | tf_op jit(solution)/shard_map/while/body/eval_jaxpr/ppermute | solution.py:9
  909.6 127.7 %reduce-scatter.2.cloned.1.call-start = ((), (), s32[]{:S(2)}) async-start(), calls=%async_computation.1 | async-start | bytes 1081344 | tf_op jit(solution)/shard_map/while/body/eval_jaxpr/reduce_scatter | solution.py:35
  920.1 117.9 %collective-permute-start = (bf16[1536,512]{1,0:T(8,128)(2,1)S(1)}, bf16[1536,512]{1,0:T(8,128)(2,1)S(1)}, u32[]{:S(2)}, u32[]{:S(2)}) collective-permute-start(bf16[1536,512]{1,0:T(8,128)(2,1)S(1)} %copy.10), channel_id=1, source_target_pairs={{0,32},{32,64},{64,96},{96,128},{128,160},{160,192},{192,224},{224... | collective-permute-start | bytes 4718600 | tf_op jit(solution)/shard_map/while/body/eval_jaxpr/ppermute | solution.py:9
Sparse Core Ops, SparseCore 0:
  18.6 119.8 reduce-scatter.1
  149.9 116.9 reduce-scatter.1
  278.4 116.6 reduce-scatter.1
  406.6 116.8 reduce-scatter.1
  534.9 116.9 reduce-scatter.1
  663.3 116.9 reduce-scatter.1
  791.8 116.9 reduce-scatter.1
  920.2 116.9 reduce-scatter.1
where the time goes:
time: 1130 us
  waiting for transfers between devices  936 us (83%)
  blocking collectives  79.7 us (7%)
  matrix products  48.4 us (4%)
  loops' own time  24.6 us (2%)
  local copies, waits for them, and re-layouts  13.6 us (1%)
  between operations  13.4 us (1%)
    reduce_scatter x8, waiting for transfers between devices, turn(): reduced = lax.psum_scatter(part, 'group', scatter_dimension=0, tiled=True)  936 us
    psum x1, blocking collectives, on_device(): total = lax.psum(column, ('blk', 'group'))  79.7 us
    dot_general x24, matrix products, panel_product(): product = jnp.dot(block, piece, preferred_element_type=jnp.float32)  48.4 us
    another operation x1, loops' own time, on_device(): unused, expanded = lax.fori_loop(0, nblock, turn, (col_values, start_out))  24.6 us
  transfers between devices with their start and end apart: 16, of which 8 were waited for; matrix products, arithmetic and copies ran while one was open for 1% of the time, Pallas kernels for 0%

commit v1 on v0

--- a/solution.py
+++ b/solution.py
@@ -41,7 +41,7 @@
     unused, expanded = lax.fori_loop(0, nblock, turn, (col_values, start_out))
     squared = expanded * expanded
     column = jnp.sum(squared, axis=0)
-    total = lax.psum(column, ("blk", "group"))
+    total = jax.lax.psum(jax.lax.psum(column, axis_name="group"), axis_name="blk")
     scale = total / (nblock * rows_here) + 1e-06
     return squared / scale
 

time: 1130 us -> 1190 us (1.053)
  blocking collectives: 79.7 us -> 139 us
    psum x1 -> x2, blocking collectives: 79.7 us -> 139 us  [the longest x1 104 us: on_device(): jax.lax.psum(column, axis_name='group')]
where the time goes in v1:
time: 1190 us; the launch traced here: 1180 us
  waiting for transfers between devices  935 us (79%)
  blocking collectives  139 us (12%)
  matrix products  48 us (4%)
  loops' own time  25.2 us (2%)
  local copies, waits for them, and re-layouts  13.6 us (1%)
  between operations  13.4 us (1%)
    reduce_scatter x8, waiting for transfers between devices, turn(): reduced = lax.psum_scatter(part, 'group', scatter_dimension=0, tiled=True)  935 us
    psum x1, blocking collectives, on_device(): jax.lax.psum(column, axis_name='group')  104 us
    dot_general x24, matrix products, panel_product(): product = jnp.dot(block, piece, preferred_element_type=jnp.float32)  48 us
    psum x1, blocking collectives, on_device(): jax.lax.psum(jax.lax.psum(column, axis_name='group'), axis_name='blk')  34.3 us
    another operation x1, loops' own time, on_device(): unused, expanded = lax.fori_loop(0, nblock, turn, (col_values, start_out))  25.2 us
  transfers between devices with their start and end apart: 16, of which 8 were waited for; matrix products, arithmetic and copies ran while one was open for 1% of the time, Pallas kernels for 0%

profile of v1, /device:TPU:1, one launch (start us, length us, event | category | flops | bytes accessed | tf_op | source)
XLA Modules:
  0.0 1183.7 jit_solution(3891503458169299501)
XLA Ops:
  6.6 1.4 copy-done
  7.9 1029.5 %while.17 = (s32[]{:T(128)}, bf16[1536,512]{1,0:T(8,128)(2,1)S(1)}, f32[16,4096]{1,0:T(8,128)S(1)}, s32[]{:T(128)}, s32[1,8]{1,0:T(1,128)S(1)}, /*index=5*/s32[3...) while((s32[]{:T(128)}, bf16[1536,512]{1,0:T(8,128)(2,1)S(1)}, ...), condition=%wide.region_2.3_spmd, body=%wide.region_0.2_spmd.sunk | while | flops 806617088 | bytes 21137560 | solution.py:41
  12.4 2.0 convolution_select_fusion.5
  14.5 1.5 convolution_select_fusion.6
  16.0 2.5 fusion.30
  18.5 2.2 collective-permute-start
  20.7 117.8 %reduce-scatter.2.cloned.1.call-done = f32[16,512]{1,0:T(8,128)} async-done(((f32[512,512]{1,0:T(8,128)}), f32[16,512]{1,0:T(8,128)}) %reduce-scatter.2.cloned.1.call-update) | async-done | bytes 32784 | tf_op jit(solution)/shard_map/while/body/eval_jaxpr/reduce_scatter | solution.py:35
  138.5 0.8 constant_dynamic-update-slice_fusion.2
  141.8 0.6 fusion.29
  143.7 2.0 convolution_select_fusion.5
  145.8 1.5 convolution_select_fusion.6
  147.3 2.5 fusion.30
  149.9 117.0 %reduce-scatter.2.cloned.1.call-done = f32[16,512]{1,0:T(8,128)} async-done(((f32[512,512]{1,0:T(8,128)}), f32[16,512]{1,0:T(8,128)}) %reduce-scatter.2.cloned.1.call-update) | async-done | bytes 32784 | tf_op jit(solution)/shard_map/while/body/eval_jaxpr/reduce_scatter | solution.py:35
  266.9 0.8 constant_dynamic-update-slice_fusion.2
  270.2 0.6 fusion.29
  272.2 2.0 convolution_select_fusion.5
  274.2 1.5 convolution_select_fusion.6
  275.7 2.5 fusion.30
  278.3 117.0 %reduce-scatter.2.cloned.1.call-done = f32[16,512]{1,0:T(8,128)} async-done(((f32[512,512]{1,0:T(8,128)}), f32[16,512]{1,0:T(8,128)}) %reduce-scatter.2.cloned.1.call-update) | async-done | bytes 32784 | tf_op jit(solution)/shard_map/while/body/eval_jaxpr/reduce_scatter | solution.py:35
  395.3 0.8 constant_dynamic-update-slice_fusion.2
  400.6 2.0 convolution_select_fusion.5
  402.6 1.5 convolution_select_fusion.6
  404.1 2.5 fusion.30
  406.7 116.7 %reduce-scatter.2.cloned.1.call-done = f32[16,512]{1,0:T(8,128)} async-done(((f32[512,512]{1,0:T(8,128)}), f32[16,512]{1,0:T(8,128)}) %reduce-scatter.2.cloned.1.call-update) | async-done | bytes 32784 | tf_op jit(solution)/shard_map/while/body/eval_jaxpr/reduce_scatter | solution.py:35
  523.4 0.8 constant_dynamic-update-slice_fusion.2
  528.7 2.0 convolution_select_fusion.5
  530.7 1.5 convolution_select_fusion.6
  532.2 2.5 fusion.30
  535.0 116.8 %reduce-scatter.2.cloned.1.call-done = f32[16,512]{1,0:T(8,128)} async-done(((f32[512,512]{1,0:T(8,128)}), f32[16,512]{1,0:T(8,128)}) %reduce-scatter.2.cloned.1.call-update) | async-done | bytes 32784 | tf_op jit(solution)/shard_map/while/body/eval_jaxpr/reduce_scatter | solution.py:35
  651.8 0.8 constant_dynamic-update-slice_fusion.2
  657.0 2.0 convolution_select_fusion.5
  659.1 1.5 convolution_select_fusion.6
  660.6 2.5 fusion.30
  663.3 117.0 %reduce-scatter.2.cloned.1.call-done = f32[16,512]{1,0:T(8,128)} async-done(((f32[512,512]{1,0:T(8,128)}), f32[16,512]{1,0:T(8,128)}) %reduce-scatter.2.cloned.1.call-update) | async-done | bytes 32784 | tf_op jit(solution)/shard_map/while/body/eval_jaxpr/reduce_scatter | solution.py:35
  780.3 0.8 constant_dynamic-update-slice_fusion.2
  785.6 2.0 convolution_select_fusion.5
  787.6 1.5 convolution_select_fusion.6
  789.1 2.5 fusion.30
  792.0 116.5 %reduce-scatter.2.cloned.1.call-done = f32[16,512]{1,0:T(8,128)} async-done(((f32[512,512]{1,0:T(8,128)}), f32[16,512]{1,0:T(8,128)}) %reduce-scatter.2.cloned.1.call-update) | async-done | bytes 32784 | tf_op jit(solution)/shard_map/while/body/eval_jaxpr/reduce_scatter | solution.py:35
  908.5 0.8 constant_dynamic-update-slice_fusion.2
  913.8 2.0 convolution_select_fusion.5
  915.8 1.5 convolution_select_fusion.6
  917.3 2.5 fusion.30
  920.2 116.5 %reduce-scatter.2.cloned.1.call-done = f32[16,512]{1,0:T(8,128)} async-done(((f32[512,512]{1,0:T(8,128)}), f32[16,512]{1,0:T(8,128)}) %reduce-scatter.2.cloned.1.call-update) | async-done | bytes 32784 | tf_op jit(solution)/shard_map/while/body/eval_jaxpr/reduce_scatter | solution.py:35
  1036.7 0.8 constant_dynamic-update-slice_fusion.2
  1037.5 104.4 %psum.14 = f32[4096]{0:T(1024)S(1)} all-reduce(f32[4096]{0:T(1024)S(1)} %multiply_reduce_fusion), channel_id=1, replica_groups=mesh['blk'=8,'group'=32] {'group'}, use_global_device_ids=true, to_apply=%region_4.5 | all-reduce | flops 4096 | bytes 32768 | tf_op jit(solution)/shard_map/psum | solution.py:44
  1141.9 34.3 %psum.15 = f32[4096]{0:T(1024)S(1)} all-reduce(f32[4096]{0:T(1024)S(1)} %psum.14), channel_id=1, replica_groups=mesh['blk'=8,'group'=32] {'blk'}, use_global_device_ids=true, to_apply=%region_5.6 | all-reduce | flops 4096 | bytes 32768 | tf_op jit(solution)/shard_map/psum | solution.py:44
  1176.2 0.7 multiply_divide_fusion
  (69 shorter events, 11.6 us)
Async XLA Ops:
  6.5 1.4 copy-start
  6.5 1.4 copy-start.1
  6.5 1.4 copy-start.2
  7.9 130.5 %reduce-scatter.2.cloned.1.call-start = ((), (), s32[]{:S(2)}) async-start(), calls=%async_computation.1 | async-start | bytes 1081344 | tf_op jit(solution)/shard_map/while/body/eval_jaxpr/reduce_scatter | solution.py:35
  18.5 120.8 %collective-permute-start = (bf16[1536,512]{1,0:T(8,128)(2,1)S(1)}, bf16[1536,512]{1,0:T(8,128)(2,1)S(1)}, u32[]{:S(2)}, u32[]{:S(2)}) collective-permute-start(bf16[1536,512]{1,0:T(8,128)(2,1)S(1)} %copy.10), channel_id=1, source_target_pairs={{0,32},{32,64},{64,96},{96,128},{128,160},{160,192},{192,224},{224... | collective-permute-start | bytes 4718600 | tf_op jit(solution)/shard_map/while/body/eval_jaxpr/ppermute | solution.py:9
  139.2 127.7 %reduce-scatter.2.cloned.1.call-start = ((), (), s32[]{:S(2)}) async-start(), calls=%async_computation.1 | async-start | bytes 1081344 | tf_op jit(solution)/shard_map/while/body/eval_jaxpr/reduce_scatter | solution.py:35
  149.8 117.9 %collective-permute-start = (bf16[1536,512]{1,0:T(8,128)(2,1)S(1)}, bf16[1536,512]{1,0:T(8,128)(2,1)S(1)}, u32[]{:S(2)}, u32[]{:S(2)}) collective-permute-start(bf16[1536,512]{1,0:T(8,128)(2,1)S(1)} %copy.10), channel_id=1, source_target_pairs={{0,32},{32,64},{64,96},{96,128},{128,160},{160,192},{192,224},{224... | collective-permute-start | bytes 4718600 | tf_op jit(solution)/shard_map/while/body/eval_jaxpr/ppermute | solution.py:9
  267.7 127.7 %reduce-scatter.2.cloned.1.call-start = ((), (), s32[]{:S(2)}) async-start(), calls=%async_computation.1 | async-start | bytes 1081344 | tf_op jit(solution)/shard_map/while/body/eval_jaxpr/reduce_scatter | solution.py:35
  278.2 117.9 %collective-permute-start = (bf16[1536,512]{1,0:T(8,128)(2,1)S(1)}, bf16[1536,512]{1,0:T(8,128)(2,1)S(1)}, u32[]{:S(2)}, u32[]{:S(2)}) collective-permute-start(bf16[1536,512]{1,0:T(8,128)(2,1)S(1)} %copy.10), channel_id=1, source_target_pairs={{0,32},{32,64},{64,96},{96,128},{128,160},{160,192},{192,224},{224... | collective-permute-start | bytes 4718600 | tf_op jit(solution)/shard_map/while/body/eval_jaxpr/ppermute | solution.py:9
  396.1 127.3 %reduce-scatter.2.cloned.1.call-start = ((), (), s32[]{:S(2)}) async-start(), calls=%async_computation.1 | async-start | bytes 1081344 | tf_op jit(solution)/shard_map/while/body/eval_jaxpr/reduce_scatter | solution.py:35
  406.6 117.6 %collective-permute-start = (bf16[1536,512]{1,0:T(8,128)(2,1)S(1)}, bf16[1536,512]{1,0:T(8,128)(2,1)S(1)}, u32[]{:S(2)}, u32[]{:S(2)}) collective-permute-start(bf16[1536,512]{1,0:T(8,128)(2,1)S(1)} %copy.10), channel_id=1, source_target_pairs={{0,32},{32,64},{64,96},{96,128},{128,160},{160,192},{192,224},{224... | collective-permute-start | bytes 4718600 | tf_op jit(solution)/shard_map/while/body/eval_jaxpr/ppermute | solution.py:9
  524.2 127.6 %reduce-scatter.2.cloned.1.call-start = ((), (), s32[]{:S(2)}) async-start(), calls=%async_computation.1 | async-start | bytes 1081344 | tf_op jit(solution)/shard_map/while/body/eval_jaxpr/reduce_scatter | solution.py:35
  534.7 117.8 %collective-permute-start = (bf16[1536,512]{1,0:T(8,128)(2,1)S(1)}, bf16[1536,512]{1,0:T(8,128)(2,1)S(1)}, u32[]{:S(2)}, u32[]{:S(2)}) collective-permute-start(bf16[1536,512]{1,0:T(8,128)(2,1)S(1)} %copy.10), channel_id=1, source_target_pairs={{0,32},{32,64},{64,96},{96,128},{128,160},{160,192},{192,224},{224... | collective-permute-start | bytes 4718600 | tf_op jit(solution)/shard_map/while/body/eval_jaxpr/ppermute | solution.py:9
  652.5 127.7 %reduce-scatter.2.cloned.1.call-start = ((), (), s32[]{:S(2)}) async-start(), calls=%async_computation.1 | async-start | bytes 1081344 | tf_op jit(solution)/shard_map/while/body/eval_jaxpr/reduce_scatter | solution.py:35
  663.1 118.0 %collective-permute-start = (bf16[1536,512]{1,0:T(8,128)(2,1)S(1)}, bf16[1536,512]{1,0:T(8,128)(2,1)S(1)}, u32[]{:S(2)}, u32[]{:S(2)}) collective-permute-start(bf16[1536,512]{1,0:T(8,128)(2,1)S(1)} %copy.10), channel_id=1, source_target_pairs={{0,32},{32,64},{64,96},{96,128},{128,160},{160,192},{192,224},{224... | collective-permute-start | bytes 4718600 | tf_op jit(solution)/shard_map/while/body/eval_jaxpr/ppermute | solution.py:9
  781.1 127.5 %reduce-scatter.2.cloned.1.call-start = ((), (), s32[]{:S(2)}) async-start(), calls=%async_computation.1 | async-start | bytes 1081344 | tf_op jit(solution)/shard_map/while/body/eval_jaxpr/reduce_scatter | solution.py:35
  791.6 117.7 %collective-permute-start = (bf16[1536,512]{1,0:T(8,128)(2,1)S(1)}, bf16[1536,512]{1,0:T(8,128)(2,1)S(1)}, u32[]{:S(2)}, u32[]{:S(2)}) collective-permute-start(bf16[1536,512]{1,0:T(8,128)(2,1)S(1)} %copy.10), channel_id=1, source_target_pairs={{0,32},{32,64},{64,96},{96,128},{128,160},{160,192},{192,224},{224... | collective-permute-start | bytes 4718600 | tf_op jit(solution)/shard_map/while/body/eval_jaxpr/ppermute | solution.py:9
  909.3 127.4 %reduce-scatter.2.cloned.1.call-start = ((), (), s32[]{:S(2)}) async-start(), calls=%async_computation.1 | async-start | bytes 1081344 | tf_op jit(solution)/shard_map/while/body/eval_jaxpr/reduce_scatter | solution.py:35
  919.8 117.6 %collective-permute-start = (bf16[1536,512]{1,0:T(8,128)(2,1)S(1)}, bf16[1536,512]{1,0:T(8,128)(2,1)S(1)}, u32[]{:S(2)}, u32[]{:S(2)}) collective-permute-start(bf16[1536,512]{1,0:T(8,128)(2,1)S(1)} %copy.10), channel_id=1, source_target_pairs={{0,32},{32,64},{64,96},{96,128},{128,160},{160,192},{192,224},{224... | collective-permute-start | bytes 4718600 | tf_op jit(solution)/shard_map/while/body/eval_jaxpr/ppermute | solution.py:9
Sparse Core Ops, SparseCore 0:
  18.6 119.8 reduce-scatter.1
  149.9 116.9 reduce-scatter.1
  278.3 116.9 reduce-scatter.1
  406.7 116.6 reduce-scatter.1
  534.8 116.9 reduce-scatter.1
  663.2 117.0 reduce-scatter.1
  791.7 116.7 reduce-scatter.1
  919.9 116.6 reduce-scatter.1
